TPU v7x, 128 devices: a whole 4x4x4 slice. The times are simulated.
128 devices in a mesh: ctx: 8 (over y, z_hi), head: 4 (over z_lo, core), dp: 4 (over x).
Axes of the slice: x: 4, y: 4, z: 4 (z_hi: 2, z_lo: 2; z = z_hi * 2 + z_lo), core: 2. Of those that a mesh axis runs over, the one named last changes fastest.
Arguments:
- long_query: bfloat16 [24576, 8192], P(('dp', 'ctx', 'head')), parts along dimension 0, may hold values from -250 to 250
- long_kv: bfloat16 [2, 24576, 1024], P(None, ('dp', 'ctx', 'head')), parts along dimension 1, may hold values from -250 to 250
- short_query: bfloat16 [32768, 8192], P(('dp', 'ctx', 'head')), parts along dimension 0, may hold values from -250 to 250
- short_key_value: bfloat16 [2, 32768, 1024], P(None, ('dp', 'ctx', 'head')), parts along dimension 1, may hold values from -250 to 250
- short_seg: int32 [128, 256], P(('dp', 'ctx', 'head')), parts along dimension 0, may hold values from 0 to 7, never falling along the last dimension, each value on 1 to 128 neighbouring positions
Outputs:
- long_out: bfloat16 [24576, 8192], P(('dp', 'ctx', 'head')), parts along dimension 0
- short_out: bfloat16 [32768, 8192], P(('dp', 'ctx', 'head')), parts along dimension 0
There are 4 independent parts, one for each index of `dp`. A program takes and returns all parts, laid end to end along the dimension named above; each array names one. Nothing has to cross between parts.
All inputs are finite; a program needn't handle non-finite values.
Results may differ from a plain program's by a relative error of at most 0.0035.
Values may be sent and summed in bfloat16 or wider, within the bound.
A program may use at most 256 MiB of HBM per device.

v0:
```python
import math
import jax
import jax.numpy as jnp
from jax import lax
from jax.sharding import PartitionSpec as P

QUERY_HEAD_COUNT = 64
KEY_VALUE_HEADS = 8
HEAD_SIZE = 128
NEG_LARGE = -1e30


def blank_state(count_of_rows, kv_heads, head_groups):
    highest = jnp.full((kv_heads, head_groups, count_of_rows), NEG_LARGE, jnp.float32)
    totals = jnp.zeros((kv_heads, head_groups, count_of_rows), jnp.float32)
    accum = jnp.zeros((kv_heads, head_groups, count_of_rows, HEAD_SIZE), jnp.float32)
    return (highest, totals, accum)


def update_state(softmax_state, query_rows, stacked_rows, allowed):
    running_max, totals, accum = softmax_state
    kv_heads = query_rows.shape[1]
    head_dim = query_rows.shape[3]
    key_part = stacked_rows[0].reshape(stacked_rows.shape[1], kv_heads, head_dim)
    value_part = stacked_rows[1].reshape(stacked_rows.shape[1], kv_heads, head_dim)
    scores = jnp.einsum(
        "tkgd,skd->kgts", query_rows, key_part, preferred_element_type=jnp.float32
    ) * (1.0 / math.sqrt(head_dim))
    masked = jnp.where(allowed, scores, NEG_LARGE)
    new_max = jnp.maximum(running_max, jnp.max(masked, axis=-1))
    factor = jnp.exp(running_max - new_max)
    weights = jnp.where(allowed, jnp.exp(scores - new_max[..., None]), 0.0)
    totals = totals * factor + jnp.sum(weights, axis=-1)
    accum = accum * factor[..., None] + jnp.einsum(
        "kgts,skd->kgtd",
        weights.astype(jnp.bfloat16),
        value_part,
        preferred_element_type=jnp.float32,
    )
    return (new_max, totals, accum)


def finish_state(softmax_state):
    running_max, totals, accum = softmax_state
    mixed = (accum / totals[..., None]).astype(jnp.bfloat16)
    return mixed.transpose(2, 0, 1, 3).reshape(mixed.shape[2], -1)


def fold_long(query_rows, query_pos, block_length):

    def fold_step(running, shard_piece, begin_at):
        turns = shard_piece.shape[1] // block_length

        def one_turn(turn_index, inner_state):
            offset = begin_at + turn_index * block_length
            part_kv = lax.dynamic_slice_in_dim(
                shard_piece, turn_index * block_length, block_length, 1
            )
            key_pos = offset + jnp.arange(block_length, dtype=jnp.int32)
            allowed = key_pos[None, :] <= query_pos[:, None]
            return lax.cond(
                offset <= query_pos[-1],
                lambda held_state: update_state(held_state, query_rows, part_kv, allowed),
                lambda held_state: held_state,
                inner_state,
            )

        return lax.fori_loop(0, turns, one_turn, running)

    return fold_step


def attend_short(short_query, short_key_value, short_seg):
    sequence_length = short_query.shape[0]
    head_groups = QUERY_HEAD_COUNT // KEY_VALUE_HEADS
    query_rows = short_query.reshape(sequence_length, KEY_VALUE_HEADS, head_groups, HEAD_SIZE)
    labels = short_seg[0]
    positions = jnp.arange(sequence_length, dtype=jnp.int32)
    block_length = sequence_length // 4
    pieces_out = []
    for query_block in range(4):
        query_low = query_block * block_length
        query_high = query_low + block_length
        softmax_state = blank_state(block_length, KEY_VALUE_HEADS, head_groups)
        for key_block in range(query_block + 1):
            key_low = key_block * block_length
            key_high = key_low + block_length
            allowed = (
                positions[key_low:key_high][None, :] <= positions[query_low:query_high][:, None]
            ) & (labels[key_low:key_high][None, :] == labels[query_low:query_high][:, None])
            softmax_state = update_state(
                softmax_state,
                query_rows[query_low:query_high],
                short_key_value[:, key_low:key_high],
                allowed,
            )
        pieces_out.append(finish_state(softmax_state))
    return jnp.concatenate(pieces_out, axis=0)


def on_device(long_query, long_kv, short_query, short_key_value, short_seg):
    token_rows = long_query.shape[0]
    head_groups = QUERY_HEAD_COUNT // KEY_VALUE_HEADS
    window_count = lax.axis_size("ctx") * lax.axis_size("head")
    flat_rank = lax.axis_index("ctx") * lax.axis_size("head") + lax.axis_index("head")
    query_rows = long_query.reshape(token_rows, KEY_VALUE_HEADS, head_groups, HEAD_SIZE)
    query_pos = flat_rank * token_rows + jnp.arange(token_rows, dtype=jnp.int32)
    shards_per_block = 1
    while shards_per_block * token_rows < 512 and shards_per_block < window_count:
        shards_per_block = shards_per_block * 2
    gathered = lax.all_gather(long_kv, ("ctx", "head"), axis=1, tiled=True)
    fold_step = fold_long(query_rows, query_pos, shards_per_block * token_rows)
    softmax_state = fold_step(blank_state(token_rows, KEY_VALUE_HEADS, head_groups), gathered, 0)
    long_out = finish_state(softmax_state)
    short_out = attend_short(short_query, short_key_value, short_seg)
    return (long_out, short_out)


def solution(mesh):
    return jax.shard_map(
        on_device,
        mesh=mesh,
        in_specs=(
            P(("dp", "ctx", "head"), None),
            P(None, ("dp", "ctx", "head"), None),
            P(("dp", "ctx", "head"), None),
            P(None, ("dp", "ctx", "head"), None),
            P(("dp", "ctx", "head"), None),
        ),
        out_specs=(P(("dp", "ctx", "head"), None), P(("dp", "ctx", "head"), None)),
        check_vma=False,
    )
```

profile of v0, /device:TPU:89, one launch (start us, length us, event | category | flops | bytes accessed | tf_op | source)
XLA Modules:
  0.0 643.4 jit_solution(1320893152180307649)
XLA Ops:
  68.7 33.4 %all-gather.2.cloned.1.call-done = bf16[2,6144,1024]{2,0,1:T(2,128)(2,1)} async-done(((bf16[2,192,1024]{2,0,1:T(2,128)(2,1)}), bf16[2,6144,1024]{2,0,1:T(2,128)(2,1)}) %all-gather.2.cloned.1.call-update) | async-done | bytes 25165840 | tf_op jit(solution)/shard_map/all_gather | solution.py:111
  102.1 60.8 %copy.70 = bf16[2,6144,1024]{1,2,0:T(8,128)(2,1)} copy(bf16[2,6144,1024]{2,0,1:T(2,128)(2,1)} %all-gather.2.cloned.1.call-done) | data formatting | bytes 50331648 | tf_op jit(solution)/shard_map/while | solution.py:68
  166.3 458.5 %while.17 = (s32[]{:T(128)}, f32[8,8,192]{2,1,0:T(8,128)S(1)}, f32[8,8,192]{2,1,0:T(8,128)S(1)}, f32[8,8,192,128]{3,2,1,0:T(8,128)}, s32[192]{0:T(256)S(1)}, /*i...) while((s32[]{:T(128)}, f32[8,8,192]{2,1,0:T(8,128)S(1)}, ...), condition=%wide.region_5.6_spmd, body=%wide.region_0.5_spmd.sunk | while | flops 4938966016 | bytes 190133392 | solution.py:68
  167.9 55.9 %conditional.2 = ((f32[8,8,192]{2,1,0:T(8,128)S(1)}, f32[8,8,192]{2,1,0:T(8,128)S(1)}, f32[8,8,192,128]{3,2,1,0:T(8,128)})) conditional(s32[]{:T(128)} %convert_element_type.108, (f32[8,8,192]{2,1,0:T(8,128)S(1)}, f32[8,8,192]{2,1,0:T(8,128)S(1)}, f32[8,8,192,128]{3,2,1,0:T(8,128)}) %tuple.107, (s32[]{:T(128)}, s32[1,768]{1,0:T(1,128)S(1)}, ...), branch_computations={%region_1.0_spmd, %region_2.4_spmd} | conditional | flops 4938966016 | bytes 190130080 | solution.py:61
  170.2 17.2 %fusion = (f32[8,8,192]{2,1,0:T(8,128)S(1)}, f32[8,768,192,8]{1,2,3,0:T(8,128)}) fusion(pred[192,768]{1,0:T(8,128)(4,1)S(1)} %broadcast_compare_fusion, bf16[768,8,128,1]{0,2,3,1:T(8,128)(2,1)S(1)} %bitcast.483, bf16[192,8,8,128]{3,0,2,1:T(8,128)(2,1)} %get-tuple-element.211), kind=kOutput, calls=%fused_computation.2 | convolution fusion | flops 2444218368 | bytes 42663936 | tf_op jit(solution)/shard_map/while/body/eval_jaxpr/cond/branch_1_fun/tkgd,skd->kgts/dot_general | solution.py:26
  187.4 17.0 %fusion.4 = f32[8,8,192]{2,1,0:T(8,128)S(1)} fusion(f32[8,768,192,8]{1,2,3,0:T(8,128)} %get-tuple-element.276, f32[8,8,192]{2,1,0:T(8,128)S(1)} %max.122, pred[192,768]{1,0:T(8,128)(4,1)S(1)} %broadcast_compare_fusion), kind=kLoop, calls=%fused_computation.6 | loop fusion | flops 37736448 | bytes 37994496 | tf_op jit(solution)/shard_map/while/body/eval_jaxpr/cond/branch_1_fun/reduce_sum | solution.py:33
  225.1 55.9 %conditional.2 = ((f32[8,8,192]{2,1,0:T(8,128)S(1)}, f32[8,8,192]{2,1,0:T(8,128)S(1)}, f32[8,8,192,128]{3,2,1,0:T(8,128)})) conditional(s32[]{:T(128)} %convert_element_type.108, (f32[8,8,192]{2,1,0:T(8,128)S(1)}, f32[8,8,192]{2,1,0:T(8,128)S(1)}, f32[8,8,192,128]{3,2,1,0:T(8,128)}) %tuple.107, (s32[]{:T(128)}, s32[1,768]{1,0:T(1,128)S(1)}, ...), branch_computations={%region_1.0_spmd, %region_2.4_spmd} | conditional | flops 4938966016 | bytes 190130080 | solution.py:61
  227.5 17.2 %fusion = (f32[8,8,192]{2,1,0:T(8,128)S(1)}, f32[8,768,192,8]{1,2,3,0:T(8,128)}) fusion(pred[192,768]{1,0:T(8,128)(4,1)S(1)} %broadcast_compare_fusion, bf16[768,8,128,1]{0,2,3,1:T(8,128)(2,1)S(1)} %bitcast.483, bf16[192,8,8,128]{3,0,2,1:T(8,128)(2,1)} %get-tuple-element.211), kind=kOutput, calls=%fused_computation.2 | convolution fusion | flops 2444218368 | bytes 42663936 | tf_op jit(solution)/shard_map/while/body/eval_jaxpr/cond/branch_1_fun/tkgd,skd->kgts/dot_general | solution.py:26
  244.6 17.0 %fusion.4 = f32[8,8,192]{2,1,0:T(8,128)S(1)} fusion(f32[8,768,192,8]{1,2,3,0:T(8,128)} %get-tuple-element.276, f32[8,8,192]{2,1,0:T(8,128)S(1)} %max.122, pred[192,768]{1,0:T(8,128)(4,1)S(1)} %broadcast_compare_fusion), kind=kLoop, calls=%fused_computation.6 | loop fusion | flops 37736448 | bytes 37994496 | tf_op jit(solution)/shard_map/while/body/eval_jaxpr/cond/branch_1_fun/reduce_sum | solution.py:33
  282.4 55.9 %conditional.2 = ((f32[8,8,192]{2,1,0:T(8,128)S(1)}, f32[8,8,192]{2,1,0:T(8,128)S(1)}, f32[8,8,192,128]{3,2,1,0:T(8,128)})) conditional(s32[]{:T(128)} %convert_element_type.108, (f32[8,8,192]{2,1,0:T(8,128)S(1)}, f32[8,8,192]{2,1,0:T(8,128)S(1)}, f32[8,8,192,128]{3,2,1,0:T(8,128)}) %tuple.107, (s32[]{:T(128)}, s32[1,768]{1,0:T(1,128)S(1)}, ...), branch_computations={%region_1.0_spmd, %region_2.4_spmd} | conditional | flops 4938966016 | bytes 190130080 | solution.py:61
  284.7 17.2 %fusion = (f32[8,8,192]{2,1,0:T(8,128)S(1)}, f32[8,768,192,8]{1,2,3,0:T(8,128)}) fusion(pred[192,768]{1,0:T(8,128)(4,1)S(1)} %broadcast_compare_fusion, bf16[768,8,128,1]{0,2,3,1:T(8,128)(2,1)S(1)} %bitcast.483, bf16[192,8,8,128]{3,0,2,1:T(8,128)(2,1)} %get-tuple-element.211), kind=kOutput, calls=%fused_computation.2 | convolution fusion | flops 2444218368 | bytes 42663936 | tf_op jit(solution)/shard_map/while/body/eval_jaxpr/cond/branch_1_fun/tkgd,skd->kgts/dot_general | solution.py:26
  301.9 17.0 %fusion.4 = f32[8,8,192]{2,1,0:T(8,128)S(1)} fusion(f32[8,768,192,8]{1,2,3,0:T(8,128)} %get-tuple-element.276, f32[8,8,192]{2,1,0:T(8,128)S(1)} %max.122, pred[192,768]{1,0:T(8,128)(4,1)S(1)} %broadcast_compare_fusion), kind=kLoop, calls=%fused_computation.6 | loop fusion | flops 37736448 | bytes 37994496 | tf_op jit(solution)/shard_map/while/body/eval_jaxpr/cond/branch_1_fun/reduce_sum | solution.py:33
  339.7 55.9 %conditional.2 = ((f32[8,8,192]{2,1,0:T(8,128)S(1)}, f32[8,8,192]{2,1,0:T(8,128)S(1)}, f32[8,8,192,128]{3,2,1,0:T(8,128)})) conditional(s32[]{:T(128)} %convert_element_type.108, (f32[8,8,192]{2,1,0:T(8,128)S(1)}, f32[8,8,192]{2,1,0:T(8,128)S(1)}, f32[8,8,192,128]{3,2,1,0:T(8,128)}) %tuple.107, (s32[]{:T(128)}, s32[1,768]{1,0:T(1,128)S(1)}, ...), branch_computations={%region_1.0_spmd, %region_2.4_spmd} | conditional | flops 4938966016 | bytes 190130080 | solution.py:61
  342.0 17.2 %fusion = (f32[8,8,192]{2,1,0:T(8,128)S(1)}, f32[8,768,192,8]{1,2,3,0:T(8,128)}) fusion(pred[192,768]{1,0:T(8,128)(4,1)S(1)} %broadcast_compare_fusion, bf16[768,8,128,1]{0,2,3,1:T(8,128)(2,1)S(1)} %bitcast.483, bf16[192,8,8,128]{3,0,2,1:T(8,128)(2,1)} %get-tuple-element.211), kind=kOutput, calls=%fused_computation.2 | convolution fusion | flops 2444218368 | bytes 42663936 | tf_op jit(solution)/shard_map/while/body/eval_jaxpr/cond/branch_1_fun/tkgd,skd->kgts/dot_general | solution.py:26
  359.2 17.0 %fusion.4 = f32[8,8,192]{2,1,0:T(8,128)S(1)} fusion(f32[8,768,192,8]{1,2,3,0:T(8,128)} %get-tuple-element.276, f32[8,8,192]{2,1,0:T(8,128)S(1)} %max.122, pred[192,768]{1,0:T(8,128)(4,1)S(1)} %broadcast_compare_fusion), kind=kLoop, calls=%fused_computation.6 | loop fusion | flops 37736448 | bytes 37994496 | tf_op jit(solution)/shard_map/while/body/eval_jaxpr/cond/branch_1_fun/reduce_sum | solution.py:33
  397.0 55.9 %conditional.2 = ((f32[8,8,192]{2,1,0:T(8,128)S(1)}, f32[8,8,192]{2,1,0:T(8,128)S(1)}, f32[8,8,192,128]{3,2,1,0:T(8,128)})) conditional(s32[]{:T(128)} %convert_element_type.108, (f32[8,8,192]{2,1,0:T(8,128)S(1)}, f32[8,8,192]{2,1,0:T(8,128)S(1)}, f32[8,8,192,128]{3,2,1,0:T(8,128)}) %tuple.107, (s32[]{:T(128)}, s32[1,768]{1,0:T(1,128)S(1)}, ...), branch_computations={%region_1.0_spmd, %region_2.4_spmd} | conditional | flops 4938966016 | bytes 190130080 | solution.py:61
  399.3 17.2 %fusion = (f32[8,8,192]{2,1,0:T(8,128)S(1)}, f32[8,768,192,8]{1,2,3,0:T(8,128)}) fusion(pred[192,768]{1,0:T(8,128)(4,1)S(1)} %broadcast_compare_fusion, bf16[768,8,128,1]{0,2,3,1:T(8,128)(2,1)S(1)} %bitcast.483, bf16[192,8,8,128]{3,0,2,1:T(8,128)(2,1)} %get-tuple-element.211), kind=kOutput, calls=%fused_computation.2 | convolution fusion | flops 2444218368 | bytes 42663936 | tf_op jit(solution)/shard_map/while/body/eval_jaxpr/cond/branch_1_fun/tkgd,skd->kgts/dot_general | solution.py:26
  416.5 17.0 %fusion.4 = f32[8,8,192]{2,1,0:T(8,128)S(1)} fusion(f32[8,768,192,8]{1,2,3,0:T(8,128)} %get-tuple-element.276, f32[8,8,192]{2,1,0:T(8,128)S(1)} %max.122, pred[192,768]{1,0:T(8,128)(4,1)S(1)} %broadcast_compare_fusion), kind=kLoop, calls=%fused_computation.6 | loop fusion | flops 37736448 | bytes 37994496 | tf_op jit(solution)/shard_map/while/body/eval_jaxpr/cond/branch_1_fun/reduce_sum | solution.py:33
  454.3 55.9 %conditional.2 = ((f32[8,8,192]{2,1,0:T(8,128)S(1)}, f32[8,8,192]{2,1,0:T(8,128)S(1)}, f32[8,8,192,128]{3,2,1,0:T(8,128)})) conditional(s32[]{:T(128)} %convert_element_type.108, (f32[8,8,192]{2,1,0:T(8,128)S(1)}, f32[8,8,192]{2,1,0:T(8,128)S(1)}, f32[8,8,192,128]{3,2,1,0:T(8,128)}) %tuple.107, (s32[]{:T(128)}, s32[1,768]{1,0:T(1,128)S(1)}, ...), branch_computations={%region_1.0_spmd, %region_2.4_spmd} | conditional | flops 4938966016 | bytes 190130080 | solution.py:61
  456.6 17.2 %fusion = (f32[8,8,192]{2,1,0:T(8,128)S(1)}, f32[8,768,192,8]{1,2,3,0:T(8,128)}) fusion(pred[192,768]{1,0:T(8,128)(4,1)S(1)} %broadcast_compare_fusion, bf16[768,8,128,1]{0,2,3,1:T(8,128)(2,1)S(1)} %bitcast.483, bf16[192,8,8,128]{3,0,2,1:T(8,128)(2,1)} %get-tuple-element.211), kind=kOutput, calls=%fused_computation.2 | convolution fusion | flops 2444218368 | bytes 42663936 | tf_op jit(solution)/shard_map/while/body/eval_jaxpr/cond/branch_1_fun/tkgd,skd->kgts/dot_general | solution.py:26
  511.6 55.9 %conditional.2 = ((f32[8,8,192]{2,1,0:T(8,128)S(1)}, f32[8,8,192]{2,1,0:T(8,128)S(1)}, f32[8,8,192,128]{3,2,1,0:T(8,128)})) conditional(s32[]{:T(128)} %convert_element_type.108, (f32[8,8,192]{2,1,0:T(8,128)S(1)}, f32[8,8,192]{2,1,0:T(8,128)S(1)}, f32[8,8,192,128]{3,2,1,0:T(8,128)}) %tuple.107, (s32[]{:T(128)}, s32[1,768]{1,0:T(1,128)S(1)}, ...), branch_computations={%region_1.0_spmd, %region_2.4_spmd} | conditional | flops 4938966016 | bytes 190130080 | solution.py:61
  513.9 17.2 %fusion = (f32[8,8,192]{2,1,0:T(8,128)S(1)}, f32[8,768,192,8]{1,2,3,0:T(8,128)}) fusion(pred[192,768]{1,0:T(8,128)(4,1)S(1)} %broadcast_compare_fusion, bf16[768,8,128,1]{0,2,3,1:T(8,128)(2,1)S(1)} %bitcast.483, bf16[192,8,8,128]{3,0,2,1:T(8,128)(2,1)} %get-tuple-element.211), kind=kOutput, calls=%fused_computation.2 | convolution fusion | flops 2444218368 | bytes 42663936 | tf_op jit(solution)/shard_map/while/body/eval_jaxpr/cond/branch_1_fun/tkgd,skd->kgts/dot_general | solution.py:26
  568.8 56.0 %conditional.2 = ((f32[8,8,192]{2,1,0:T(8,128)S(1)}, f32[8,8,192]{2,1,0:T(8,128)S(1)}, f32[8,8,192,128]{3,2,1,0:T(8,128)})) conditional(s32[]{:T(128)} %convert_element_type.108, (f32[8,8,192]{2,1,0:T(8,128)S(1)}, f32[8,8,192]{2,1,0:T(8,128)S(1)}, f32[8,8,192,128]{3,2,1,0:T(8,128)}) %tuple.107, (s32[]{:T(128)}, s32[1,768]{1,0:T(1,128)S(1)}, ...), branch_computations={%region_1.0_spmd, %region_2.4_spmd} | conditional | flops 4938966016 | bytes 190130080 | solution.py:61
  571.2 17.2 %fusion = (f32[8,8,192]{2,1,0:T(8,128)S(1)}, f32[8,768,192,8]{1,2,3,0:T(8,128)}) fusion(pred[192,768]{1,0:T(8,128)(4,1)S(1)} %broadcast_compare_fusion, bf16[768,8,128,1]{0,2,3,1:T(8,128)(2,1)S(1)} %bitcast.483, bf16[192,8,8,128]{3,0,2,1:T(8,128)(2,1)} %get-tuple-element.211), kind=kOutput, calls=%fused_computation.2 | convolution fusion | flops 2444218368 | bytes 42663936 | tf_op jit(solution)/shard_map/while/body/eval_jaxpr/cond/branch_1_fun/tkgd,skd->kgts/dot_general | solution.py:26
  (194 shorter events, 305.5 us)
Async XLA Ops:
  7.2 95.0 %all-gather.2.cloned.1.call-start = ((), (), s32[]{:S(2)}) async-start(), calls=%async_computation | async-start | bytes 25952256 | tf_op jit(solution)/shard_map/all_gather | solution.py:111
  12.8 3.9 copy-start.2
  16.6 0.6 copy-start.5
  17.1 1.2 copy-start.3
  18.3 0.7 copy-start.4
  18.4 0.8 slice-start
  187.3 17.1 %copy-start = (f32[8,8,192,128]{3,2,1,0:T(8,128)S(1)}, f32[8,8,192,128]{3,2,1,0:T(8,128)}, u32[]{:S(2)}) copy-start(f32[8,8,192,128]{3,2,1,0:T(8,128)} %get-tuple-element.213) | copy-start | bytes 18874372 | tf_op jit(solution)/shard_map/while/body/eval_jaxpr/cond
  221.2 2.6 copy-start.1
  244.6 17.1 %copy-start = (f32[8,8,192,128]{3,2,1,0:T(8,128)S(1)}, f32[8,8,192,128]{3,2,1,0:T(8,128)}, u32[]{:S(2)}) copy-start(f32[8,8,192,128]{3,2,1,0:T(8,128)} %get-tuple-element.213) | copy-start | bytes 18874372 | tf_op jit(solution)/shard_map/while/body/eval_jaxpr/cond
  278.4 2.6 copy-start.1
  301.9 17.1 %copy-start = (f32[8,8,192,128]{3,2,1,0:T(8,128)S(1)}, f32[8,8,192,128]{3,2,1,0:T(8,128)}, u32[]{:S(2)}) copy-start(f32[8,8,192,128]{3,2,1,0:T(8,128)} %get-tuple-element.213) | copy-start | bytes 18874372 | tf_op jit(solution)/shard_map/while/body/eval_jaxpr/cond
  335.7 2.6 copy-start.1
  359.2 17.1 %copy-start = (f32[8,8,192,128]{3,2,1,0:T(8,128)S(1)}, f32[8,8,192,128]{3,2,1,0:T(8,128)}, u32[]{:S(2)}) copy-start(f32[8,8,192,128]{3,2,1,0:T(8,128)} %get-tuple-element.213) | copy-start | bytes 18874372 | tf_op jit(solution)/shard_map/while/body/eval_jaxpr/cond
  393.0 2.6 copy-start.1
  416.5 17.1 %copy-start = (f32[8,8,192,128]{3,2,1,0:T(8,128)S(1)}, f32[8,8,192,128]{3,2,1,0:T(8,128)}, u32[]{:S(2)}) copy-start(f32[8,8,192,128]{3,2,1,0:T(8,128)} %get-tuple-element.213) | copy-start | bytes 18874372 | tf_op jit(solution)/shard_map/while/body/eval_jaxpr/cond
  450.3 2.6 copy-start.1
  473.7 17.1 %copy-start = (f32[8,8,192,128]{3,2,1,0:T(8,128)S(1)}, f32[8,8,192,128]{3,2,1,0:T(8,128)}, u32[]{:S(2)}) copy-start(f32[8,8,192,128]{3,2,1,0:T(8,128)} %get-tuple-element.213) | copy-start | bytes 18874372 | tf_op jit(solution)/shard_map/while/body/eval_jaxpr/cond
  507.6 2.6 copy-start.1
  531.0 17.1 %copy-start = (f32[8,8,192,128]{3,2,1,0:T(8,128)S(1)}, f32[8,8,192,128]{3,2,1,0:T(8,128)}, u32[]{:S(2)}) copy-start(f32[8,8,192,128]{3,2,1,0:T(8,128)} %get-tuple-element.213) | copy-start | bytes 18874372 | tf_op jit(solution)/shard_map/while/body/eval_jaxpr/cond
  564.9 2.6 copy-start.1
  588.4 17.1 %copy-start = (f32[8,8,192,128]{3,2,1,0:T(8,128)S(1)}, f32[8,8,192,128]{3,2,1,0:T(8,128)}, u32[]{:S(2)}) copy-start(f32[8,8,192,128]{3,2,1,0:T(8,128)} %get-tuple-element.213) | copy-start | bytes 18874372 | tf_op jit(solution)/shard_map/while/body/eval_jaxpr/cond
  622.2 2.6 copy-start.1
Sparse Core Ops, SparseCore 0:
  10.2 91.8 all-gather.1
where the time goes:
time: 656 us; the launch traced here: 643 us
  matrix products  302 us (46%)
  other arithmetic  153 us (23%)
  local copies, waits for them, and re-layouts  133 us (20%)
  waiting for transfers between devices  33.4 us (5%)
  between operations  14.9 us (2%)
  loops' own time  6.58 us (1%)
    dot_general x18, matrix products, update_state(): jnp.einsum('tkgd,skd->kgts', query_rows, key_part, preferred_element_type...  153 us
    dot_general x18, matrix products, update_state(): jnp.einsum('kgts,skd->kgtd', weights.astype(jnp.bfloat16), value_part, pr...  149 us
    reduce_sum x13, other arithmetic, update_state(): totals = totals * factor + jnp.sum(weights, axis=-1)  143 us
    while x2, local copies, waits for them, and re-layouts, fold_step(): return lax.fori_loop(0, turns, one_turn, running)  64.4 us
    all_gather x1, waiting for transfers between devices, on_device(): gathered = lax.all_gather(long_kv, ('ctx', 'head'), axis=1, tiled=True)  33.4 us
    cond x40, local copies, waits for them, and re-layouts  21 us
    unnamed x29, local copies, waits for them, and re-layouts  17 us
    slice x8, local copies, waits for them, and re-layouts, update_state(): stacked_rows[1].reshape(stacked_rows.shape[1], kv_heads, head_dim)  16.9 us
  transfers between devices with their start and end apart: 1, of which 1 were waited for; matrix products, arithmetic and copies ran while one was open for 9% of the time, Pallas kernels for 0%

commit v1 on v0

--- a/solution.py
+++ b/solution.py
@@ -108,7 +108,11 @@
     shards_per_block = 1
     while shards_per_block * token_rows < 512 and shards_per_block < window_count:
         shards_per_block = shards_per_block * 2
-    gathered = lax.all_gather(long_kv, ("ctx", "head"), axis=1, tiled=True)
+    before = tuple((long_kv for _ in range(lax.axis_size(("ctx", "head")))))
+    side_arr = lax.all_to_all(
+        jnp.stack(before, axis=0), concat_axis=0, split_axis=0, axis_name=("ctx", "head")
+    )
+    gathered = jnp.concatenate(side_arr, axis=1)
     fold_step = fold_long(query_rows, query_pos, shards_per_block * token_rows)
     softmax_state = fold_step(blank_state(token_rows, KEY_VALUE_HEADS, head_groups), gathered, 0)
     long_out = finish_state(softmax_state)

time: 656 us -> 901 us (1.37)
  the two profiles are of different devices: /device:TPU:89 before, /device:TPU:125 now
where the time goes in v1:
time: 901 us; the launch traced here: 889 us
  matrix products  302 us (34%)
  waiting for transfers between devices  287 us (32%)
  other arithmetic  153 us (17%)
  local copies, waits for them, and re-layouts  131 us (15%)
    all_to_all x1, waiting for transfers between devices, on_device(): lax.all_to_all(jnp.stack(before, axis=0), concat_axis=0, split_axis=0, ax...  287 us
    dot_general x18, matrix products, update_state(): jnp.einsum('tkgd,skd->kgts', query_rows, key_part, preferred_element_type...  153 us
    dot_general x18, matrix products, update_state(): jnp.einsum('kgts,skd->kgtd', weights.astype(jnp.bfloat16), value_part, pr...  149 us
    reduce_sum x13, other arithmetic, update_state(): totals = totals * factor + jnp.sum(weights, axis=-1)  143 us
    while x2, local copies, waits for them, and re-layouts, fold_step(): return lax.fori_loop(0, turns, one_turn, running)  36.4 us
    cond x40, local copies, waits for them, and re-layouts  21.3 us
    all_to_all x1, local copies, waits for them, and re-layouts, on_device(): lax.all_to_all(jnp.stack(before, axis=0), concat_axis=0, split_axis=0, ax...  21 us
  transfers between devices with their start and end apart: 1, of which 1 were waited for; matrix products, arithmetic and copies ran while one was open for 6% of the time, Pallas kernels for 0%

profile of v1, /device:TPU:125, one launch (start us, length us, event | category | flops | bytes accessed | tf_op | source)
XLA Modules:
  0.0 888.8 jit_solution(9188883630036323506)
XLA Ops:
  74.5 287.0 %all-to-all-done = bf16[32,2,192,1024]{3,2,1,0:T(8,128)(2,1)} async-done(((bf16[32,2,192,1024]{3,2,1,0:T(8,128)(2,1)}), bf16[32,2,192,1024]{3,2,1,0:T(8,128)(2,1)}, u32[]{:S(2)}, u32[]{:S(2)}) %all-to-all-start) | async-done | bytes 25165856 | tf_op jit(solution)/shard_map/all_to_all | solution.py:112
  361.4 21.0 %copy.118 = bf16[32,2,192,1024]{3,2,0,1:T(8,128)(2,1)} copy(bf16[32,2,192,1024]{3,2,1,0:T(8,128)(2,1)} %all-to-all-done) | data formatting | bytes 50331648 | tf_op jit(solution)/shard_map/all_to_all | solution.py:112
  382.4 32.8 %copy.119 = bf16[2,6144,1024]{1,2,0:T(8,128)(2,1)} copy(bf16[2,6144,1024]{2,1,0:T(8,128)(2,1)} %bitcast.487) | data formatting | bytes 50331648 | tf_op jit(solution)/shard_map/while | solution.py:68
  418.6 458.5 %while.17 = (s32[]{:T(128)}, f32[8,8,192]{2,1,0:T(8,128)S(1)}, f32[8,8,192]{2,1,0:T(8,128)S(1)}, f32[8,8,192,128]{3,2,1,0:T(8,128)}, s32[192]{0:T(256)S(1)}, /*i...) while((s32[]{:T(128)}, f32[8,8,192]{2,1,0:T(8,128)S(1)}, ...), condition=%wide.region_5.6_spmd, body=%wide.region_0.5_spmd.sunk | while | flops 4938966016 | bytes 190133392 | solution.py:68
  420.2 55.9 %conditional.2 = ((f32[8,8,192]{2,1,0:T(8,128)S(1)}, f32[8,8,192]{2,1,0:T(8,128)S(1)}, f32[8,8,192,128]{3,2,1,0:T(8,128)})) conditional(s32[]{:T(128)} %convert_element_type.108, (f32[8,8,192]{2,1,0:T(8,128)S(1)}, f32[8,8,192]{2,1,0:T(8,128)S(1)}, f32[8,8,192,128]{3,2,1,0:T(8,128)}) %tuple.108, (s32[]{:T(128)}, s32[1,768]{1,0:T(1,128)S(1)}, ...), branch_computations={%region_1.0_spmd, %region_2.4_spmd} | conditional | flops 4938966016 | bytes 190130080 | solution.py:61
  422.5 17.1 %fusion = (f32[8,8,192]{2,1,0:T(8,128)S(1)}, f32[8,768,192,8]{1,2,3,0:T(8,128)}) fusion(pred[192,768]{1,0:T(8,128)(4,1)S(1)} %broadcast_compare_fusion, bf16[768,8,128,1]{0,2,3,1:T(8,128)(2,1)S(1)} %bitcast.486, bf16[192,8,8,128]{3,0,2,1:T(8,128)(2,1)} %get-tuple-element.211), kind=kOutput, calls=%fused_computation.2 | convolution fusion | flops 2444218368 | bytes 42663936 | tf_op jit(solution)/shard_map/while/body/eval_jaxpr/cond/branch_1_fun/tkgd,skd->kgts/dot_general | solution.py:26
  439.6 17.0 %fusion.4 = f32[8,8,192]{2,1,0:T(8,128)S(1)} fusion(f32[8,768,192,8]{1,2,3,0:T(8,128)} %get-tuple-element.283, f32[8,8,192]{2,1,0:T(8,128)S(1)} %max.122, pred[192,768]{1,0:T(8,128)(4,1)S(1)} %broadcast_compare_fusion), kind=kLoop, calls=%fused_computation.6 | loop fusion | flops 37736448 | bytes 37994496 | tf_op jit(solution)/shard_map/while/body/eval_jaxpr/cond/branch_1_fun/reduce_sum | solution.py:33
  477.5 55.9 %conditional.2 = ((f32[8,8,192]{2,1,0:T(8,128)S(1)}, f32[8,8,192]{2,1,0:T(8,128)S(1)}, f32[8,8,192,128]{3,2,1,0:T(8,128)})) conditional(s32[]{:T(128)} %convert_element_type.108, (f32[8,8,192]{2,1,0:T(8,128)S(1)}, f32[8,8,192]{2,1,0:T(8,128)S(1)}, f32[8,8,192,128]{3,2,1,0:T(8,128)}) %tuple.108, (s32[]{:T(128)}, s32[1,768]{1,0:T(1,128)S(1)}, ...), branch_computations={%region_1.0_spmd, %region_2.4_spmd} | conditional | flops 4938966016 | bytes 190130080 | solution.py:61
  479.8 17.1 %fusion = (f32[8,8,192]{2,1,0:T(8,128)S(1)}, f32[8,768,192,8]{1,2,3,0:T(8,128)}) fusion(pred[192,768]{1,0:T(8,128)(4,1)S(1)} %broadcast_compare_fusion, bf16[768,8,128,1]{0,2,3,1:T(8,128)(2,1)S(1)} %bitcast.486, bf16[192,8,8,128]{3,0,2,1:T(8,128)(2,1)} %get-tuple-element.211), kind=kOutput, calls=%fused_computation.2 | convolution fusion | flops 2444218368 | bytes 42663936 | tf_op jit(solution)/shard_map/while/body/eval_jaxpr/cond/branch_1_fun/tkgd,skd->kgts/dot_general | solution.py:26
  496.9 17.0 %fusion.4 = f32[8,8,192]{2,1,0:T(8,128)S(1)} fusion(f32[8,768,192,8]{1,2,3,0:T(8,128)} %get-tuple-element.283, f32[8,8,192]{2,1,0:T(8,128)S(1)} %max.122, pred[192,768]{1,0:T(8,128)(4,1)S(1)} %broadcast_compare_fusion), kind=kLoop, calls=%fused_computation.6 | loop fusion | flops 37736448 | bytes 37994496 | tf_op jit(solution)/shard_map/while/body/eval_jaxpr/cond/branch_1_fun/reduce_sum | solution.py:33
  534.7 55.9 %conditional.2 = ((f32[8,8,192]{2,1,0:T(8,128)S(1)}, f32[8,8,192]{2,1,0:T(8,128)S(1)}, f32[8,8,192,128]{3,2,1,0:T(8,128)})) conditional(s32[]{:T(128)} %convert_element_type.108, (f32[8,8,192]{2,1,0:T(8,128)S(1)}, f32[8,8,192]{2,1,0:T(8,128)S(1)}, f32[8,8,192,128]{3,2,1,0:T(8,128)}) %tuple.108, (s32[]{:T(128)}, s32[1,768]{1,0:T(1,128)S(1)}, ...), branch_computations={%region_1.0_spmd, %region_2.4_spmd} | conditional | flops 4938966016 | bytes 190130080 | solution.py:61
  537.1 17.1 %fusion = (f32[8,8,192]{2,1,0:T(8,128)S(1)}, f32[8,768,192,8]{1,2,3,0:T(8,128)}) fusion(pred[192,768]{1,0:T(8,128)(4,1)S(1)} %broadcast_compare_fusion, bf16[768,8,128,1]{0,2,3,1:T(8,128)(2,1)S(1)} %bitcast.486, bf16[192,8,8,128]{3,0,2,1:T(8,128)(2,1)} %get-tuple-element.211), kind=kOutput, calls=%fused_computation.2 | convolution fusion | flops 2444218368 | bytes 42663936 | tf_op jit(solution)/shard_map/while/body/eval_jaxpr/cond/branch_1_fun/tkgd,skd->kgts/dot_general | solution.py:26
  554.2 17.0 %fusion.4 = f32[8,8,192]{2,1,0:T(8,128)S(1)} fusion(f32[8,768,192,8]{1,2,3,0:T(8,128)} %get-tuple-element.283, f32[8,8,192]{2,1,0:T(8,128)S(1)} %max.122, pred[192,768]{1,0:T(8,128)(4,1)S(1)} %broadcast_compare_fusion), kind=kLoop, calls=%fused_computation.6 | loop fusion | flops 37736448 | bytes 37994496 | tf_op jit(solution)/shard_map/while/body/eval_jaxpr/cond/branch_1_fun/reduce_sum | solution.py:33
  592.0 55.9 %conditional.2 = ((f32[8,8,192]{2,1,0:T(8,128)S(1)}, f32[8,8,192]{2,1,0:T(8,128)S(1)}, f32[8,8,192,128]{3,2,1,0:T(8,128)})) conditional(s32[]{:T(128)} %convert_element_type.108, (f32[8,8,192]{2,1,0:T(8,128)S(1)}, f32[8,8,192]{2,1,0:T(8,128)S(1)}, f32[8,8,192,128]{3,2,1,0:T(8,128)}) %tuple.108, (s32[]{:T(128)}, s32[1,768]{1,0:T(1,128)S(1)}, ...), branch_computations={%region_1.0_spmd, %region_2.4_spmd} | conditional | flops 4938966016 | bytes 190130080 | solution.py:61
  594.3 17.1 %fusion = (f32[8,8,192]{2,1,0:T(8,128)S(1)}, f32[8,768,192,8]{1,2,3,0:T(8,128)}) fusion(pred[192,768]{1,0:T(8,128)(4,1)S(1)} %broadcast_compare_fusion, bf16[768,8,128,1]{0,2,3,1:T(8,128)(2,1)S(1)} %bitcast.486, bf16[192,8,8,128]{3,0,2,1:T(8,128)(2,1)} %get-tuple-element.211), kind=kOutput, calls=%fused_computation.2 | convolution fusion | flops 2444218368 | bytes 42663936 | tf_op jit(solution)/shard_map/while/body/eval_jaxpr/cond/branch_1_fun/tkgd,skd->kgts/dot_general | solution.py:26
  611.5 17.0 %fusion.4 = f32[8,8,192]{2,1,0:T(8,128)S(1)} fusion(f32[8,768,192,8]{1,2,3,0:T(8,128)} %get-tuple-element.283, f32[8,8,192]{2,1,0:T(8,128)S(1)} %max.122, pred[192,768]{1,0:T(8,128)(4,1)S(1)} %broadcast_compare_fusion), kind=kLoop, calls=%fused_computation.6 | loop fusion | flops 37736448 | bytes 37994496 | tf_op jit(solution)/shard_map/while/body/eval_jaxpr/cond/branch_1_fun/reduce_sum | solution.py:33
  649.3 55.9 %conditional.2 = ((f32[8,8,192]{2,1,0:T(8,128)S(1)}, f32[8,8,192]{2,1,0:T(8,128)S(1)}, f32[8,8,192,128]{3,2,1,0:T(8,128)})) conditional(s32[]{:T(128)} %convert_element_type.108, (f32[8,8,192]{2,1,0:T(8,128)S(1)}, f32[8,8,192]{2,1,0:T(8,128)S(1)}, f32[8,8,192,128]{3,2,1,0:T(8,128)}) %tuple.108, (s32[]{:T(128)}, s32[1,768]{1,0:T(1,128)S(1)}, ...), branch_computations={%region_1.0_spmd, %region_2.4_spmd} | conditional | flops 4938966016 | bytes 190130080 | solution.py:61
  651.6 17.1 %fusion = (f32[8,8,192]{2,1,0:T(8,128)S(1)}, f32[8,768,192,8]{1,2,3,0:T(8,128)}) fusion(pred[192,768]{1,0:T(8,128)(4,1)S(1)} %broadcast_compare_fusion, bf16[768,8,128,1]{0,2,3,1:T(8,128)(2,1)S(1)} %bitcast.486, bf16[192,8,8,128]{3,0,2,1:T(8,128)(2,1)} %get-tuple-element.211), kind=kOutput, calls=%fused_computation.2 | convolution fusion | flops 2444218368 | bytes 42663936 | tf_op jit(solution)/shard_map/while/body/eval_jaxpr/cond/branch_1_fun/tkgd,skd->kgts/dot_general | solution.py:26
  706.6 55.9 %conditional.2 = ((f32[8,8,192]{2,1,0:T(8,128)S(1)}, f32[8,8,192]{2,1,0:T(8,128)S(1)}, f32[8,8,192,128]{3,2,1,0:T(8,128)})) conditional(s32[]{:T(128)} %convert_element_type.108, (f32[8,8,192]{2,1,0:T(8,128)S(1)}, f32[8,8,192]{2,1,0:T(8,128)S(1)}, f32[8,8,192,128]{3,2,1,0:T(8,128)}) %tuple.108, (s32[]{:T(128)}, s32[1,768]{1,0:T(1,128)S(1)}, ...), branch_computations={%region_1.0_spmd, %region_2.4_spmd} | conditional | flops 4938966016 | bytes 190130080 | solution.py:61
  708.9 17.1 %fusion = (f32[8,8,192]{2,1,0:T(8,128)S(1)}, f32[8,768,192,8]{1,2,3,0:T(8,128)}) fusion(pred[192,768]{1,0:T(8,128)(4,1)S(1)} %broadcast_compare_fusion, bf16[768,8,128,1]{0,2,3,1:T(8,128)(2,1)S(1)} %bitcast.486, bf16[192,8,8,128]{3,0,2,1:T(8,128)(2,1)} %get-tuple-element.211), kind=kOutput, calls=%fused_computation.2 | convolution fusion | flops 2444218368 | bytes 42663936 | tf_op jit(solution)/shard_map/while/body/eval_jaxpr/cond/branch_1_fun/tkgd,skd->kgts/dot_general | solution.py:26
  763.9 55.9 %conditional.2 = ((f32[8,8,192]{2,1,0:T(8,128)S(1)}, f32[8,8,192]{2,1,0:T(8,128)S(1)}, f32[8,8,192,128]{3,2,1,0:T(8,128)})) conditional(s32[]{:T(128)} %convert_element_type.108, (f32[8,8,192]{2,1,0:T(8,128)S(1)}, f32[8,8,192]{2,1,0:T(8,128)S(1)}, f32[8,8,192,128]{3,2,1,0:T(8,128)}) %tuple.108, (s32[]{:T(128)}, s32[1,768]{1,0:T(1,128)S(1)}, ...), branch_computations={%region_1.0_spmd, %region_2.4_spmd} | conditional | flops 4938966016 | bytes 190130080 | solution.py:61
  766.2 17.1 %fusion = (f32[8,8,192]{2,1,0:T(8,128)S(1)}, f32[8,768,192,8]{1,2,3,0:T(8,128)}) fusion(pred[192,768]{1,0:T(8,128)(4,1)S(1)} %broadcast_compare_fusion, bf16[768,8,128,1]{0,2,3,1:T(8,128)(2,1)S(1)} %bitcast.486, bf16[192,8,8,128]{3,0,2,1:T(8,128)(2,1)} %get-tuple-element.211), kind=kOutput, calls=%fused_computation.2 | convolution fusion | flops 2444218368 | bytes 42663936 | tf_op jit(solution)/shard_map/while/body/eval_jaxpr/cond/branch_1_fun/tkgd,skd->kgts/dot_general | solution.py:26
  821.2 55.9 %conditional.2 = ((f32[8,8,192]{2,1,0:T(8,128)S(1)}, f32[8,8,192]{2,1,0:T(8,128)S(1)}, f32[8,8,192,128]{3,2,1,0:T(8,128)})) conditional(s32[]{:T(128)} %convert_element_type.108, (f32[8,8,192]{2,1,0:T(8,128)S(1)}, f32[8,8,192]{2,1,0:T(8,128)S(1)}, f32[8,8,192,128]{3,2,1,0:T(8,128)}) %tuple.108, (s32[]{:T(128)}, s32[1,768]{1,0:T(1,128)S(1)}, ...), branch_computations={%region_1.0_spmd, %region_2.4_spmd} | conditional | flops 4938966016 | bytes 190130080 | solution.py:61
  823.5 17.1 %fusion = (f32[8,8,192]{2,1,0:T(8,128)S(1)}, f32[8,768,192,8]{1,2,3,0:T(8,128)}) fusion(pred[192,768]{1,0:T(8,128)(4,1)S(1)} %broadcast_compare_fusion, bf16[768,8,128,1]{0,2,3,1:T(8,128)(2,1)S(1)} %bitcast.486, bf16[192,8,8,128]{3,0,2,1:T(8,128)(2,1)} %get-tuple-element.211), kind=kOutput, calls=%fused_computation.2 | convolution fusion | flops 2444218368 | bytes 42663936 | tf_op jit(solution)/shard_map/while/body/eval_jaxpr/cond/branch_1_fun/tkgd,skd->kgts/dot_general | solution.py:26
  (196 shorter events, 335.0 us)
Async XLA Ops:
  10.1 7.7 copy-start.3
  10.1 351.3 %all-to-all-start = ((bf16[32,2,192,1024]{3,2,1,0:T(8,128)(2,1)}), bf16[32,2,192,1024]{3,2,1,0:T(8,128)(2,1)}, u32[]{:S(2)}, u32[]{:S(2)}) async-start(bf16[32,2,192,1024]{3,2,1,0:T(8,128)(2,1)} %stack.2), calls=%async_computation | async-start | bytes 50331648 | tf_op jit(solution)/shard_map/all_to_all | solution.py:112
  18.7 3.9 copy-start.2
  22.4 0.6 copy-start.6
  23.0 1.2 copy-start.4
  24.2 0.7 copy-start.5
  24.2 0.8 slice-start
  439.6 17.1 %copy-start = (f32[8,8,192,128]{3,2,1,0:T(8,128)S(1)}, f32[8,8,192,128]{3,2,1,0:T(8,128)}, u32[]{:S(2)}) copy-start(f32[8,8,192,128]{3,2,1,0:T(8,128)} %get-tuple-element.213) | copy-start | bytes 18874372 | tf_op jit(solution)/shard_map/while/body/eval_jaxpr/cond
  473.4 2.7 copy-start.1
  496.9 17.1 %copy-start = (f32[8,8,192,128]{3,2,1,0:T(8,128)S(1)}, f32[8,8,192,128]{3,2,1,0:T(8,128)}, u32[]{:S(2)}) copy-start(f32[8,8,192,128]{3,2,1,0:T(8,128)} %get-tuple-element.213) | copy-start | bytes 18874372 | tf_op jit(solution)/shard_map/while/body/eval_jaxpr/cond
  530.7 2.7 copy-start.1
  554.2 17.1 %copy-start = (f32[8,8,192,128]{3,2,1,0:T(8,128)S(1)}, f32[8,8,192,128]{3,2,1,0:T(8,128)}, u32[]{:S(2)}) copy-start(f32[8,8,192,128]{3,2,1,0:T(8,128)} %get-tuple-element.213) | copy-start | bytes 18874372 | tf_op jit(solution)/shard_map/while/body/eval_jaxpr/cond
  588.0 2.7 copy-start.1
  611.5 17.1 %copy-start = (f32[8,8,192,128]{3,2,1,0:T(8,128)S(1)}, f32[8,8,192,128]{3,2,1,0:T(8,128)}, u32[]{:S(2)}) copy-start(f32[8,8,192,128]{3,2,1,0:T(8,128)} %get-tuple-element.213) | copy-start | bytes 18874372 | tf_op jit(solution)/shard_map/while/body/eval_jaxpr/cond
  645.3 2.7 copy-start.1
  668.8 17.1 %copy-start = (f32[8,8,192,128]{3,2,1,0:T(8,128)S(1)}, f32[8,8,192,128]{3,2,1,0:T(8,128)}, u32[]{:S(2)}) copy-start(f32[8,8,192,128]{3,2,1,0:T(8,128)} %get-tuple-element.213) | copy-start | bytes 18874372 | tf_op jit(solution)/shard_map/while/body/eval_jaxpr/cond
  702.6 2.7 copy-start.1
  726.0 17.1 %copy-start = (f32[8,8,192,128]{3,2,1,0:T(8,128)S(1)}, f32[8,8,192,128]{3,2,1,0:T(8,128)}, u32[]{:S(2)}) copy-start(f32[8,8,192,128]{3,2,1,0:T(8,128)} %get-tuple-element.213) | copy-start | bytes 18874372 | tf_op jit(solution)/shard_map/while/body/eval_jaxpr/cond
  759.9 2.7 copy-start.1
  783.3 17.1 %copy-start = (f32[8,8,192,128]{3,2,1,0:T(8,128)S(1)}, f32[8,8,192,128]{3,2,1,0:T(8,128)}, u32[]{:S(2)}) copy-start(f32[8,8,192,128]{3,2,1,0:T(8,128)} %get-tuple-element.213) | copy-start | bytes 18874372 | tf_op jit(solution)/shard_map/while/body/eval_jaxpr/cond
  817.2 2.7 copy-start.1
  840.6 17.1 %copy-start = (f32[8,8,192,128]{3,2,1,0:T(8,128)S(1)}, f32[8,8,192,128]{3,2,1,0:T(8,128)}, u32[]{:S(2)}) copy-start(f32[8,8,192,128]{3,2,1,0:T(8,128)} %get-tuple-element.213) | copy-start | bytes 18874372 | tf_op jit(solution)/shard_map/while/body/eval_jaxpr/cond
  874.4 2.7 copy-start.1
